TPU v7x, 32 devices: a whole 2x2x4 slice. The times are simulated.
32 devices in a mesh: arc: 2 (over y), trow: 4 (over z), tcol: 4 (over x, core).
Axes of the slice: x: 2, y: 2, z: 4, core: 2. Of those that a mesh axis runs over, the one named last changes fastest.
Arguments:
- design: bfloat16 [1280, 8192], P('arc', 'tcol'), may hold values from -0.25 to 0.25
- local_design: bfloat16 [1280, 128], P('arc'), may hold values from -0.3125 to 0.3125
- lengths: int32 [4], P('arc'), may hold values from 1 to 320, 960 in all
- regularizer: float32 [8192], P(('arc', 'trow')), may hold values from 0.2 to 2
Outputs:
- normal: float32 [8192, 8192], P(('arc', 'trow'), 'tcol')
- panel_factor: float32 [2, 8192, 512], P(None, 'tcol')
Inputs may be any that keep to these rules, and one draw needn't show every extreme that they name: `lengths`: each arc has at least one live row; some arc is full.
All inputs are finite; a program needn't handle non-finite values. No bound on the sum of `lengths` on one device may be relied on, other than what follows from the above.
Results may differ from a plain program's by a relative error of at most 0.003.
Values may be sent and summed in bfloat16 or wider, within the bound.
No kernel may reach another device: no remote copies, remote signals or barrier semaphores. Data moves between devices by JAX's collectives and lax.ppermute only.
A program may use at most 128 MiB of HBM per device.

v0:
```python
import jax
import jax.numpy as jnp
from jax import lax
from jax.sharding import PartitionSpec as P

PANEL = 512
PANELS = 2
ridge = 0.1


def broadcast(block, axis, holder):
    block = jnp.where(lax.axis_index(axis) == holder, block, jnp.zeros_like(block))
    return lax.psum(block, axis)


def project_arcs(design, local_design, lengths):
    arc_count = lengths.shape[0]
    row_count = design.shape[0]
    capacity = row_count // arc_count
    arc_blocks = design.reshape(arc_count, capacity, design.shape[1])
    local_half = local_design.reshape(arc_count, capacity, local_design.shape[1])
    live_rows = jnp.arange(capacity, dtype=jnp.int32)[None, :] < lengths[:, None]
    arc_blocks = jnp.where(live_rows[:, :, None], arc_blocks, jnp.zeros((), design.dtype))
    local_half = jnp.where(live_rows[:, :, None], local_half, jnp.zeros((), local_design.dtype))
    local_normal = jnp.einsum(
        "acl,acm->alm", local_half, local_half, preferred_element_type=jnp.float32
    )
    local_normal = local_normal + ridge * jnp.eye(local_half.shape[2], dtype=jnp.float32)[None]
    local_factor = jnp.linalg.cholesky(local_normal)
    local_cols = local_half.astype(jnp.float32)
    basis_rows = lax.linalg.triangular_solve(
        local_factor, jnp.transpose(local_cols, (0, 2, 1)), left_side=True, lower=True
    )
    basis_rows = basis_rows.astype(jnp.bfloat16)
    loadings = jnp.einsum(
        "alc,acw->alw", basis_rows, arc_blocks, preferred_element_type=jnp.float32
    ).astype(jnp.bfloat16)
    cleaned = arc_blocks.astype(jnp.float32) - jnp.einsum(
        "alc,alw->acw", basis_rows, loadings, preferred_element_type=jnp.float32
    )
    return cleaned.astype(jnp.bfloat16).reshape(row_count, design.shape[1])


def contract_rows(left_rows, right_rows):
    return lax.dot_general(
        left_rows, right_rows, (((0,), (0,)), ((), ())), preferred_element_type=jnp.float32
    )


def per_device(design, local_design, lengths, regularizer):
    row_count, col_width = design.shape
    tile_rows = regularizer.shape[0]
    arc_total = lax.axis_size("arc")
    trow_total = lax.axis_size("trow")
    trow_index = lax.axis_index("trow")
    row_start = (lax.axis_index("arc") * trow_total + trow_index) * tile_rows
    col_start = lax.axis_index("tcol") * col_width
    projected = project_arcs(design, local_design, lengths)
    gathered = lax.all_gather(projected, "tcol", axis=1, tiled=True)
    regrouped = gathered.reshape(row_count, arc_total, trow_total, tile_rows)
    selected = lax.dynamic_slice_in_dim(regrouped, trow_index, 1, 2).reshape(
        row_count, arc_total * tile_rows
    )
    received = lax.all_to_all(selected, "arc", split_axis=1, concat_axis=0, tiled=True)
    normal_block = contract_rows(received, lax.all_gather(projected, "arc", axis=0, tiled=True))
    rows_global = row_start + jnp.arange(tile_rows, dtype=jnp.int32)
    cols_global = col_start + jnp.arange(col_width, dtype=jnp.int32)
    on_diagonal = rows_global[:, None] == cols_global[None, :]
    normal_block = normal_block + jnp.where(
        on_diagonal, regularizer[:, None], jnp.zeros((), jnp.float32)
    )
    panel_factors = []
    for panel_index in range(PANELS):
        lead_col = panel_index * PANEL
        padded_rows = jnp.pad(normal_block, ((PANEL, PANEL), (0, 0)))
        slice_start = jnp.clip(lead_col - row_start + PANEL, 0, tile_rows + PANEL)
        slice_rows = lax.dynamic_slice_in_dim(padded_rows, slice_start, PANEL, 0)
        panel_global = lead_col + jnp.arange(PANEL, dtype=jnp.int32)
        in_tile = (panel_global >= row_start) & (panel_global < row_start + tile_rows)
        own_share = jnp.where(in_tile[:, None], slice_rows, jnp.zeros((), jnp.float32))
        panel_strip = lax.psum(own_share, ("arc", "trow"))
        pivot_block, row_strip = (
            broadcast(panel_strip[:, lead_col : lead_col + PANEL], "tcol", 0),
            broadcast(normal_block[:, lead_col : lead_col + PANEL], "tcol", 0),
        )
        lower_factor = jnp.linalg.cholesky(pivot_block)
        col_factor = lax.linalg.triangular_solve(
            lower_factor, panel_strip, left_side=True, lower=True
        ).T
        row_factor = lax.linalg.triangular_solve(
            lower_factor, row_strip.T, left_side=True, lower=True
        ).T
        col_factor = jnp.where(
            cols_global[:, None] >= lead_col, col_factor, jnp.zeros((), jnp.float32)
        )
        row_factor = jnp.where(
            rows_global[:, None] >= lead_col, row_factor, jnp.zeros((), jnp.float32)
        )
        normal_block = normal_block - jnp.dot(
            row_factor, col_factor.T, precision=lax.Precision.HIGHEST
        )
        panel_factors.append(col_factor)
    return (normal_block, jnp.stack(panel_factors))


def solution(mesh):
    return jax.shard_map(
        per_device,
        mesh=mesh,
        in_specs=(P("arc", "tcol"), P("arc", None), P("arc"), P(("arc", "trow"))),
        out_specs=(P(("arc", "trow"), "tcol"), P(None, "tcol", None)),
        check_vma=False,
    )
```

profile of v0, /device:TPU:0, one launch (start us, length us, event | category | flops | bytes accessed | tf_op | source)
XLA Modules:
  0.0 1101.1 jit_solution(17169129062626182126)
XLA Ops:
  9.6 23.5 %custom-call.33 = f32[2,128,128]{2,1,0:T(8,128)S(1)} custom-call(f32[2,128,128]{2,1,0:T(8,128)S(1)} %fusion.105), custom_call_target="Cholesky" | custom-call | tf_op jit(solution)/shard_map/jit(cholesky)/cholesky | solution.py:29
  33.4 19.7 %custom-call.34 = f32[2,1,128,128]{2,3,1,0:T(8,128)S(1)} custom-call(f32[2,1,128,128]{3,2,1,0:T(8,128)S(1)} %select_bitcast_fusion), custom_call_target="InvertDiagBlocksLowerTriangular" | custom-call | tf_op jit(solution)/shard_map/triangular_solve | solution.py:31
  62.1 72.3 %all-gather.3.cloned.1.call-done = bf16[640,8192]{0,1:T(8,128)(2,1)} async-done(((bf16[640,2048]{0,1:T(8,128)(2,1)}), bf16[640,8192]{0,1:T(8,128)(2,1)}) %all-gather.3.cloned.1.call-update) | async-done | bytes 10485776 | tf_op jit(solution)/shard_map/all_gather | solution.py:59
  143.5 87.0 %all-gather.5.cloned.1.call-done = bf16[1280,2048]{1,0:T(8,128)(2,1)} async-done(((bf16[640,2048]{1,0:T(8,128)(2,1)}), bf16[1280,2048]{1,0:T(8,128)(2,1)}) %all-gather.5.cloned.1.call-update) | async-done | bytes 5242896 | tf_op jit(solution)/shard_map/all_gather | solution.py:65
  248.4 152.4 %all-reduce.10.cloned.1.call-done = f32[512,2048]{0,1:T(8,128)} async-done(((f32[512,2048]{0,1:T(8,128)}), f32[512,2048]{0,1:T(8,128)}) %all-reduce.10.cloned.1.call-update) | async-done | bytes 4194320 | tf_op jit(solution)/shard_map/psum | solution.py:81
  403.2 67.9 %all-reduce.16.cloned.1.call-done = (f32[512,512]{0,1:T(8,128)}, f32[512,1024]{1,0:T(8,128)}) async-done(((f32[512,512]{0,1:T(8,128)}, f32[512,1024]{1,0:T(8,128)}), (f32[512,512]{0,1:T(8,128)}, f32[512,1024]{1,0:T(8,128)})) %all-reduce.16.cloned.1.call-update) | async-done | bytes 3145744 | tf_op jit(solution)/shard_map/psum | solution.py:13
  474.1 11.7 %cholesky.327 = f32[128,128]{1,0:T(8,128)S(1)} custom-call(f32[128,128]{1,0:T(8,128)S(1)} %cholesky.467), custom_call_target="Cholesky" | custom-call | tf_op jit(solution)/shard_map/jit(cholesky)/cholesky | solution.py:86
  496.5 11.7 %cholesky.346 = f32[128,128]{1,0:T(8,128)S(1)} custom-call(f32[128,128]{1,0:T(8,128)S(1)} %cholesky.471), custom_call_target="Cholesky" | custom-call | tf_op jit(solution)/shard_map/jit(cholesky)/cholesky | solution.py:86
  508.2 10.0 custom-call.41
  518.8 11.7 %cholesky.367 = f32[128,128]{1,0:T(8,128)S(1)} custom-call(f32[128,128]{1,0:T(8,128)S(1)} %cholesky.476), custom_call_target="Cholesky" | custom-call | tf_op jit(solution)/shard_map/jit(cholesky)/cholesky | solution.py:86
  530.6 9.8 custom-call.42
  541.0 11.7 %cholesky.384 = f32[128,128]{1,0:T(8,128)S(1)} custom-call(f32[128,128]{1,0:T(8,128)S(1)} %convolution_subtract_fusion.15), custom_call_target="Cholesky" | custom-call | tf_op jit(solution)/shard_map/jit(cholesky)/cholesky | solution.py:86
  566.2 39.3 %custom-call.43 = f32[4,128,128]{1,2,0:T(8,128)S(1)} custom-call(f32[4,128,128]{2,1,0:T(8,128)S(1)} %get-tuple-element.33), custom_call_target="InvertDiagBlocksLowerTriangular" | custom-call | tf_op jit(solution)/shard_map/triangular_solve/custom-call.9 | solution.py:90
  639.3 15.1 %convolution_subtract_fusion.1 = f32[1024,2048]{0,1:T(8,128)S(1)} fusion(f32[1024,2048]{0,1:T(8,128)S(1)} %bitcast.164, f32[128,2048]{0,1:T(8,128)S(1)} %fusion.128, f32[128,2048]{0,1:T(8,128)S(1)} %copy-done.4, f32[128,2048]{0,1:T(8,128)S(1)} %copy-done.3, f32[128,2048]{0,1:T(8,128)S(1)} %copy.71, f32[128,1024]{1,0:T(8,128)S(1)} %fusion.129, ...), kind=kOutput, calls=%fused_computation.14 | convolution fusion | flops 12893290496 | bytes 23071744 | tf_op jit(solution)/shard_map/dot_general | solution.py:99
  664.2 153.4 %all-reduce.12.cloned.1.call-done = f32[512,2048]{0,1:T(8,128)} async-done(((f32[512,2048]{0,1:T(8,128)}), f32[512,2048]{0,1:T(8,128)}) %all-reduce.12.cloned.1.call-update) | async-done | bytes 4194320 | tf_op jit(solution)/shard_map/psum | solution.py:81
  823.6 64.4 %all-reduce.14.cloned.1.call-done = (f32[512,512]{0,1:T(8,128)}, f32[512,1024]{1,0:T(8,128)}) async-done(((f32[512,512]{0,1:T(8,128)}, f32[512,1024]{1,0:T(8,128)}), (f32[512,512]{0,1:T(8,128)}, f32[512,1024]{1,0:T(8,128)})) %all-reduce.14.cloned.1.call-update) | async-done | bytes 3145744 | tf_op jit(solution)/shard_map/psum | solution.py:13
  891.0 11.7 %cholesky.399 = f32[128,128]{1,0:T(8,128)S(1)} custom-call(f32[128,128]{1,0:T(8,128)S(1)} %cholesky.480), custom_call_target="Cholesky" | custom-call | tf_op jit(solution)/shard_map/jit(cholesky)/cholesky | solution.py:86
  913.4 11.7 %cholesky.418 = f32[128,128]{1,0:T(8,128)S(1)} custom-call(f32[128,128]{1,0:T(8,128)S(1)} %cholesky.484), custom_call_target="Cholesky" | custom-call | tf_op jit(solution)/shard_map/jit(cholesky)/cholesky | solution.py:86
  925.1 10.0 custom-call.46
  935.8 11.7 %cholesky.439 = f32[128,128]{1,0:T(8,128)S(1)} custom-call(f32[128,128]{1,0:T(8,128)S(1)} %cholesky.489), custom_call_target="Cholesky" | custom-call | tf_op jit(solution)/shard_map/jit(cholesky)/cholesky | solution.py:86
  947.5 9.8 custom-call.47
  957.9 11.7 %cholesky.456 = f32[128,128]{1,0:T(8,128)S(1)} custom-call(f32[128,128]{1,0:T(8,128)S(1)} %convolution_subtract_fusion.14), custom_call_target="Cholesky" | custom-call | tf_op jit(solution)/shard_map/jit(cholesky)/cholesky | solution.py:86
  983.6 39.3 %custom-call.48 = f32[4,128,128]{1,2,0:T(8,128)S(1)} custom-call(f32[4,128,128]{2,1,0:T(8,128)S(1)} %get-tuple-element.35), custom_call_target="InvertDiagBlocksLowerTriangular" | custom-call | tf_op jit(solution)/shard_map/triangular_solve/custom-call.9 | solution.py:90
  1060.6 16.5 %convolution_subtract_fusion = f32[1024,2048]{0,1:T(8,128)} fusion(f32[1024,2048]{0,1:T(8,128)S(1)} %bitcast.162, f32[128,2048]{0,1:T(8,128)S(1)} %fusion.134, f32[128,2048]{0,1:T(8,128)S(1)} %copy-done.7, f32[128,2048]{0,1:T(8,128)S(1)} %copy-done.6, f32[128,2048]{0,1:T(8,128)S(1)} %copy.80, f32[128,1024]{1,0:T(8,128)S(1)} %fusion.135, ...), kind=kOutput, calls=%fused_computation.13 | convolution fusion | flops 12893290496 | bytes 23071744 | tf_op jit(solution)/shard_map/dot_general | solution.py:99
  (192 shorter events, 212.8 us)
Async XLA Ops:
  7.2 127.3 %all-gather.3.cloned.1.call-start = ((), (), s32[]{:S(2)}) async-start(), calls=%async_computation.1 | async-start | bytes 13107200 | tf_op jit(solution)/shard_map/all_gather | solution.py:59
  58.4 3.1 copy-start.2
  61.4 169.1 %all-gather.5.cloned.1.call-start = ((), (), s32[]{:S(2)}) async-start(), calls=%async_computation.2 | async-start | bytes 7864320 | tf_op jit(solution)/shard_map/all_gather | solution.py:65
  136.4 94.1 %copy-start.12 = (f32[1024]{0:T(1024)S(1)}, f32[1024]{0:T(1024)}, u32[]{:S(2)}) copy-start(f32[1024]{0:T(1024)} %param.12) | copy-start | bytes 12292
  139.0 91.4 %all-to-all-start = ((bf16[640,2,1024]{2,0,1:T(8,128)(2,1)}), bf16[640,2,1024]{2,0,1:T(8,128)(2,1)S(1)}, u32[]{:S(2)}, u32[]{:S(2)}) async-start(bf16[640,2,1024]{2,0,1:T(8,128)(2,1)} %bitcast.7), calls=%async_computation | async-start | bytes 5242880 | tf_op jit(solution)/shard_map/all_to_all | solution.py:64
  142.9 257.8 %all-reduce.10.cloned.1.call-start = ((), (), s32[]{:S(2)}) async-start(), calls=%async_computation.3 | async-start | bytes 8388608 | tf_op jit(solution)/shard_map/psum | solution.py:81
  238.5 3.4 copy-start.1
  245.1 226.0 %all-reduce.16.cloned.1.call-start = ((), (), s32[]{:S(2)}) async-start(), calls=%async_computation.6 | async-start | bytes 6291456 | tf_op jit(solution)/shard_map/psum | solution.py:13
  403.0 414.6 %all-reduce.12.cloned.1.call-start = ((), (), s32[]{:S(2)}) async-start(), calls=%async_computation.4 | async-start | bytes 8388608 | tf_op jit(solution)/shard_map/psum | solution.py:81
  566.2 42.0 %copy-start.9 = (f32[512,512]{1,0:T(8,128)}, f32[512,512]{1,0:T(8,128)S(1)}, u32[]{:S(2)}) copy-start(f32[512,512]{1,0:T(8,128)S(1)} %get-tuple-element.210) | copy-start | bytes 3145732
  623.1 8.3 copy-start.10
  623.1 16.2 %slice-start.2 = ((s8[8388608]{0:T(1024)(128)(4,1)}), s8[4194304]{0:T(1024)(128)(4,1)S(1)}, s32[]{:S(2)}) async-start(s8[8388608]{0:T(1024)(128)(4,1)} %bitcast.163), calls=%async_computation.9 | async-start | bytes 8388608
  631.4 7.9 copy-start.5
  632.1 7.2 slice-start.3
  633.7 5.7 copy-start.3
  633.7 5.7 copy-start.4
  654.4 3.4 copy-start
  661.0 227.0 %all-reduce.14.cloned.1.call-start = ((), (), s32[]{:S(2)}) async-start(), calls=%async_computation.5 | async-start | bytes 6291456 | tf_op jit(solution)/shard_map/psum | solution.py:13
  983.6 42.0 %copy-start.8 = (f32[512,512]{1,0:T(8,128)}, f32[512,512]{1,0:T(8,128)S(1)}, u32[]{:S(2)}) copy-start(f32[512,512]{1,0:T(8,128)S(1)} %get-tuple-element.209) | copy-start | bytes 3145732
  1040.5 8.6 copy-start.11
  1051.1 5.8 copy-start.6
  1051.1 5.8 copy-start.7
  1051.7 7.5 slice-start
  1056.9 3.7 slice-start.1
Sparse Core Ops, SparseCore 0:
  61.5 72.8 all-gather.2
  136.5 93.8 all-gather.4
  245.2 155.4 all-reduce.9
  403.6 67.4 all-reduce.15
  661.1 156.4 all-reduce.11
  820.5 67.4 all-reduce.13
where the time goes:
time: 1110 us; the launch traced here: 1100 us
  waiting for transfers between devices  598 us (54%)
  other arithmetic  316 us (28%)
  matrix products  109 us (10%)
  local copies, waits for them, and re-layouts  52.6 us (5%)
  between operations  20.3 us (2%)
    psum x2, waiting for transfers between devices, per_device(): panel_strip = lax.psum(own_share, ('arc', 'trow'))  306 us
    another operation x30, other arithmetic, per_device(): lower_factor = jnp.linalg.cholesky(pivot_block)  158 us
    psum x2, waiting for transfers between devices, broadcast(): return lax.psum(block, axis)  132 us
    all_gather x1, waiting for transfers between devices, per_device(): lax.all_gather(projected, 'arc', axis=0, tiled=True)  87 us
    another operation x5, other arithmetic, per_device(): lax.linalg.triangular_solve(lower_factor, row_strip.T, left_side=True, lo...  79.5 us
    all_gather x1, waiting for transfers between devices, per_device(): gathered = lax.all_gather(projected, 'tcol', axis=1, tiled=True)  72.3 us
    another operation x14, matrix products, per_device(): lax.linalg.triangular_solve(lower_factor, panel_strip, left_side=True, lo...  43.5 us
    dot_general x2, matrix products, per_device(): jnp.dot(row_factor, col_factor.T, precision=lax.Precision.HIGHEST)  31.6 us
  transfers between devices with their start and end apart: 7, of which 6 were waited for; matrix products, arithmetic and copies ran while one was open for 1% of the time, Pallas kernels for 0%

commit v1 on v0

--- a/solution.py
+++ b/solution.py
@@ -10,7 +10,11 @@
 
 def broadcast(block, axis, holder):
     block = jnp.where(lax.axis_index(axis) == holder, block, jnp.zeros_like(block))
-    return lax.psum(block, axis)
+
+    def get_the_counts(vec, dev_axis):
+        return lax.all_gather(vec, axis_name=dev_axis).sum(axis=0)
+
+    return get_the_counts(block, axis)
 
 
 def project_arcs(design, local_design, lengths):

time: 1110 us -> 1040 us (0.937)
  waiting for transfers between devices: 598 us -> 529 us
  other arithmetic: 316 us -> 333 us
  matrix products: 109 us -> 95.2 us
    psum x2 -> x0, waiting for transfers between devices: 132 us -> none  [broadcast(): return lax.psum(block, axis)]
    all_gather x0 -> x4, waiting for transfers between devices: none -> 56.5 us  [get_the_counts(): return lax.all_gather(vec, axis_name=dev_axis).sum(axis=0)]
    another operation x14, matrix products: 43.5 us -> 25 us  [per_device(): lax.linalg.triangular_solve(lower_factor, panel_strip, left_side=True, lo...]
    reduce_sum x0 -> x4, other arithmetic: none -> 17.5 us  [get_the_counts(): return lax.all_gather(vec, axis_name=dev_axis).sum(axis=0)]
  transfers between devices with their start and end apart: 7 -> 9, of which waited for: 6 -> 6; matrix products, arithmetic and copies ran while one was open for 1% -> 32% of each run, Pallas kernels for 0% -> 0%
where the time goes in v1:
time: 1040 us; the launch traced here: 1030 us
  waiting for transfers between devices  529 us (51%)
  other arithmetic  333 us (32%)
  matrix products  95.2 us (9%)
  local copies, waits for them, and re-layouts  49.3 us (5%)
  between operations  20.7 us (2%)
    psum x2, waiting for transfers between devices, per_device(): panel_strip = lax.psum(own_share, ('arc', 'trow'))  312 us
    another operation x30, other arithmetic, per_device(): lower_factor = jnp.linalg.cholesky(pivot_block)  168 us
    all_gather x1, waiting for transfers between devices, per_device(): lax.all_gather(projected, 'arc', axis=0, tiled=True)  87.2 us
    another operation x5, other arithmetic, per_device(): lax.linalg.triangular_solve(lower_factor, row_strip.T, left_side=True, lo...  78.9 us
    all_gather x1, waiting for transfers between devices, per_device(): gathered = lax.all_gather(projected, 'tcol', axis=1, tiled=True)  72.3 us
    all_gather x4, waiting for transfers between devices, get_the_counts(): return lax.all_gather(vec, axis_name=dev_axis).sum(axis=0)  56.5 us
    dot_general x2, matrix products, per_device(): jnp.dot(row_factor, col_factor.T, precision=lax.Precision.HIGHEST)  33.9 us
    another operation x14, matrix products, per_device(): lax.linalg.triangular_solve(lower_factor, panel_strip, left_side=True, lo...  25 us
  transfers between devices with their start and end apart: 9, of which 6 were waited for; matrix products, arithmetic and copies ran while one was open for 32% of the time, Pallas kernels for 0%

profile of v1, /device:TPU:0, one launch (start us, length us, event | category | flops | bytes accessed | tf_op | source)
XLA Modules:
  0.0 1031.8 jit_solution(8989303528737078301)
XLA Ops:
  9.6 23.5 %custom-call.33 = f32[2,128,128]{2,1,0:T(8,128)S(1)} custom-call(f32[2,128,128]{2,1,0:T(8,128)S(1)} %fusion.103), custom_call_target="Cholesky" | custom-call | tf_op jit(solution)/shard_map/jit(cholesky)/cholesky | solution.py:33
  33.4 19.7 %custom-call.34 = f32[2,1,128,128]{2,3,1,0:T(8,128)S(1)} custom-call(f32[2,1,128,128]{3,2,1,0:T(8,128)S(1)} %select_bitcast_fusion), custom_call_target="InvertDiagBlocksLowerTriangular" | custom-call | tf_op jit(solution)/shard_map/triangular_solve | solution.py:35
  62.1 72.3 %all-gather.11.cloned.1.call-done = bf16[640,8192]{0,1:T(8,128)(2,1)} async-done(((bf16[640,2048]{0,1:T(8,128)(2,1)}), bf16[640,8192]{0,1:T(8,128)(2,1)}) %all-gather.11.cloned.1.call-update) | async-done | bytes 10485776 | tf_op jit(solution)/shard_map/all_gather | solution.py:63
  143.2 87.2 %all-gather.13.cloned.1.call-done = bf16[1280,2048]{1,0:T(8,128)(2,1)} async-done(((bf16[640,2048]{1,0:T(8,128)(2,1)}), bf16[1280,2048]{1,0:T(8,128)(2,1)}) %all-gather.13.cloned.1.call-update) | async-done | bytes 5242896 | tf_op jit(solution)/shard_map/all_gather | solution.py:69
  244.2 155.6 %all-reduce.6.cloned.1.call-done = f32[512,2048]{1,0:T(8,128)} async-done(((f32[512,2048]{1,0:T(8,128)}), f32[512,2048]{1,0:T(8,128)}) %all-reduce.6.cloned.1.call-update) | async-done | bytes 4194320 | tf_op jit(solution)/shard_map/psum | solution.py:85
  405.4 30.3 %all-gather.15.cloned.1.call-done = f32[2048,512]{1,0:T(8,128)} async-done(((f32[512,512]{1,0:T(8,128)}), f32[2048,512]{1,0:T(8,128)}) %all-gather.15.cloned.1.call-update) | async-done | bytes 4194320 | tf_op jit(solution)/shard_map/all_gather | solution.py:15
  439.1 11.7 %cholesky.327 = f32[128,128]{1,0:T(8,128)S(1)} custom-call(f32[128,128]{1,0:T(8,128)S(1)} %cholesky.467), custom_call_target="Cholesky" | custom-call | tf_op jit(solution)/shard_map/jit(cholesky)/cholesky | solution.py:90
  461.4 11.7 %cholesky.346 = f32[128,128]{1,0:T(8,128)S(1)} custom-call(f32[128,128]{1,0:T(8,128)S(1)} %cholesky.471), custom_call_target="Cholesky" | custom-call | tf_op jit(solution)/shard_map/jit(cholesky)/cholesky | solution.py:90
  473.2 18.5 %custom-call.41 = f32[1,128,128]{1,2,0:T(8,128)S(1)} custom-call(f32[1,128,128]{2,1,0:T(8,128)S(1)} %get-tuple-element.83), custom_call_target="InvertDiagBlocksLowerTriangular" | custom-call | tf_op jit(solution)/shard_map/jit(cholesky)/cholesky | solution.py:90
  492.4 11.7 %cholesky.367 = f32[128,128]{1,0:T(8,128)S(1)} custom-call(f32[128,128]{1,0:T(8,128)S(1)} %cholesky.476), custom_call_target="Cholesky" | custom-call | tf_op jit(solution)/shard_map/jit(cholesky)/cholesky | solution.py:90
  504.1 9.8 custom-call.42
  514.6 12.1 %cholesky.384 = f32[128,128]{1,0:T(8,128)S(1)} custom-call(f32[128,128]{1,0:T(8,128)S(1)} %convolution_subtract_fusion.15), custom_call_target="Cholesky" | custom-call | tf_op jit(solution)/shard_map/jit(cholesky)/cholesky | solution.py:90
  540.8 39.3 %custom-call.43 = f32[4,128,128]{1,2,0:T(8,128)S(1)} custom-call(f32[4,128,128]{2,1,0:T(8,128)S(1)} %get-tuple-element.33), custom_call_target="InvertDiagBlocksLowerTriangular" | custom-call | tf_op jit(solution)/shard_map/triangular_solve/custom-call.9 | solution.py:94
  611.4 16.9 %convolution_subtract_fusion.1 = f32[1024,2048]{1,0:T(8,128)S(1)} fusion(f32[1024,2048]{1,0:T(8,128)} %copy-done.1, f32[128,2048]{1,0:T(8,128)S(1)} %copy-done.4, f32[128,2048]{1,0:T(8,128)S(1)} %fusion.124, f32[128,2048]{1,0:T(8,128)S(1)} %fusion.122, f32[128,2048]{1,0:T(8,128)S(1)} %fusion.66, f32[128,1024]{1,0:T(8,128)S(1)} %fusion.127, ...), kind=kOutput, calls=%fused_computation.14 | convolution fusion | flops 12893290496 | bytes 23071744 | tf_op jit(solution)/shard_map/dot_general | solution.py:103
  634.4 156.5 %all-reduce.8.cloned.1.call-done = f32[512,2048]{1,0:T(8,128)} async-done(((f32[512,2048]{1,0:T(8,128)}), f32[512,2048]{1,0:T(8,128)}) %all-reduce.8.cloned.1.call-update) | async-done | bytes 4194320 | tf_op jit(solution)/shard_map/psum | solution.py:85
  800.6 26.2 %all-gather.19.cloned.1.call-done = f32[2048,512]{1,0:T(8,128)} async-done(((f32[512,512]{1,0:T(8,128)}), f32[2048,512]{1,0:T(8,128)}) %all-gather.19.cloned.1.call-update) | async-done | bytes 4194320 | tf_op jit(solution)/shard_map/all_gather | solution.py:15
  830.2 11.7 %cholesky.399 = f32[128,128]{1,0:T(8,128)S(1)} custom-call(f32[128,128]{1,0:T(8,128)S(1)} %cholesky.480), custom_call_target="Cholesky" | custom-call | tf_op jit(solution)/shard_map/jit(cholesky)/cholesky | solution.py:90
  852.5 11.9 %cholesky.418 = f32[128,128]{1,0:T(8,128)S(1)} custom-call(f32[128,128]{1,0:T(8,128)S(1)} %cholesky.484), custom_call_target="Cholesky" | custom-call | tf_op jit(solution)/shard_map/jit(cholesky)/cholesky | solution.py:90
  864.4 9.8 custom-call.46
  874.9 11.7 %cholesky.439 = f32[128,128]{1,0:T(8,128)S(1)} custom-call(f32[128,128]{1,0:T(8,128)S(1)} %cholesky.489), custom_call_target="Cholesky" | custom-call | tf_op jit(solution)/shard_map/jit(cholesky)/cholesky | solution.py:90
  886.7 9.8 custom-call.47
  897.1 11.9 %cholesky.456 = f32[128,128]{1,0:T(8,128)S(1)} custom-call(f32[128,128]{1,0:T(8,128)S(1)} %convolution_subtract_fusion.14), custom_call_target="Cholesky" | custom-call | tf_op jit(solution)/shard_map/jit(cholesky)/cholesky | solution.py:90
  922.2 39.3 %custom-call.48 = f32[4,128,128]{1,2,0:T(8,128)S(1)} custom-call(f32[4,128,128]{2,1,0:T(8,128)S(1)} %get-tuple-element.35), custom_call_target="InvertDiagBlocksLowerTriangular" | custom-call | tf_op jit(solution)/shard_map/triangular_solve/custom-call.9 | solution.py:94
  1007.6 16.9 %convolution_subtract_fusion = f32[1024,2048]{1,0:T(8,128)} fusion(f32[1024,2048]{1,0:T(8,128)} %copy-done, f32[128,2048]{1,0:T(8,128)S(1)} %copy-done.6, f32[128,2048]{1,0:T(8,128)S(1)} %fusion.130, f32[128,2048]{1,0:T(8,128)S(1)} %fusion.128, f32[128,2048]{1,0:T(8,128)S(1)} %fusion.64, f32[128,1024]{1,0:T(8,128)S(1)} %fusion.133, ...), kind=kOutput, calls=%fused_computation.13 | convolution fusion | flops 12893290496 | bytes 23071744 | tf_op jit(solution)/shard_map/dot_general | solution.py:103
  (190 shorter events, 201.2 us)
Async XLA Ops:
  7.2 127.3 %all-gather.11.cloned.1.call-start = ((), (), s32[]{:S(2)}) async-start(), calls=%async_computation.1 | async-start | bytes 13107200 | tf_op jit(solution)/shard_map/all_gather | solution.py:63
  58.4 3.1 copy-start.3
  61.4 169.1 %all-gather.13.cloned.1.call-start = ((), (), s32[]{:S(2)}) async-start(), calls=%async_computation.2 | async-start | bytes 7864320 | tf_op jit(solution)/shard_map/all_gather | solution.py:69
  136.4 94.1 %copy-start.13 = (f32[1024]{0:T(1024)S(1)}, f32[1024]{0:T(1024)}, u32[]{:S(2)}) copy-start(f32[1024]{0:T(1024)} %param.12) | copy-start | bytes 12292
  139.0 91.4 %all-to-all-start = ((bf16[640,2,1024]{2,0,1:T(8,128)(2,1)}), bf16[640,2,1024]{2,0,1:T(8,128)(2,1)S(1)}, u32[]{:S(2)}, u32[]{:S(2)}) async-start(bf16[640,2,1024]{2,0,1:T(8,128)(2,1)} %bitcast.7), calls=%async_computation | async-start | bytes 5242880 | tf_op jit(solution)/shard_map/all_to_all | solution.py:68
  142.9 256.9 %all-reduce.6.cloned.1.call-start = ((), (), s32[]{:S(2)}) async-start(), calls=%async_computation.3 | async-start | bytes 8388608 | tf_op jit(solution)/shard_map/psum | solution.py:85
  238.1 3.4 copy-start.1
  244.2 191.6 %all-gather.15.cloned.1.call-start = ((), (), s32[]{:S(2)}) async-start(), calls=%async_computation.5 | async-start | bytes 5242880 | tf_op jit(solution)/shard_map/all_gather | solution.py:15
  402.1 191.0 %all-gather.17.cloned.1.call-start = ((), (), s32[]{:S(2)}) async-start(), calls=%async_computation.6 | async-start | bytes 10485760 | tf_op jit(solution)/shard_map/all_gather | solution.py:15
  405.3 385.5 %all-reduce.8.cloned.1.call-start = ((), (), s32[]{:S(2)}) async-start(), calls=%async_computation.4 | async-start | bytes 8388608 | tf_op jit(solution)/shard_map/psum | solution.py:85
  540.8 45.1 %copy-start.12 = (f32[512,512]{1,0:T(8,128)}, f32[512,512]{1,0:T(8,128)S(1)}, u32[]{:S(2)}) copy-start(f32[512,512]{1,0:T(8,128)S(1)} %get-tuple-element.206) | copy-start | bytes 3145732
  580.1 5.7 copy-start.9
  602.2 4.2 copy-start.7
  605.7 5.6 copy-start.4
  628.3 3.4 copy-start
  634.3 192.5 %all-gather.19.cloned.1.call-start = ((), (), s32[]{:S(2)}) async-start(), calls=%async_computation.7 | async-start | bytes 5242880 | tf_op jit(solution)/shard_map/all_gather | solution.py:15
  793.2 196.3 %all-gather.21.cloned.1.call-start = ((), (), s32[]{:S(2)}) async-start(), calls=%async_computation.8 | async-start | bytes 10485760 | tf_op jit(solution)/shard_map/all_gather | solution.py:15
  922.2 45.1 %copy-start.11 = (f32[512,512]{1,0:T(8,128)}, f32[512,512]{1,0:T(8,128)S(1)}, u32[]{:S(2)}) copy-start(f32[512,512]{1,0:T(8,128)S(1)} %get-tuple-element.205) | copy-start | bytes 3145732
  961.5 5.7 copy-start.10
  973.6 1.0 copy-start.5
  974.6 2.2 copy-start.2
  998.5 4.2 copy-start.8
  1002.0 5.6 copy-start.6
Sparse Core Ops, SparseCore 0:
  61.5 72.8 all-gather.10
  136.5 93.8 all-gather.12
  244.3 155.4 all-reduce.5
  402.2 33.4 all-gather.14
  437.7 58.2 all-gather.16
  634.5 156.3 all-reduce.7
  793.3 33.4 all-gather.18
  828.4 58.3 all-gather.20
